TPU v7x, 512 devices: a whole 4x8x8 slice. The times are simulated.
512 devices in a mesh: req: 32 (over y, x), exp: 16 (over z, core).
Axes of the slice: x: 4, y: 8, z: 8, core: 2. Of those that a mesh axis runs over, the one named last changes fastest.
Arguments:
- resid_in: bfloat16 [4096, 3584], P(('req', 'exp')), may hold values from -6 to 6
- queries: bfloat16 [4096, 3584], P(('req', 'exp')), may hold values from -40 to 40
- fresh_kv: bfloat16 [4096, 1024], P(('req', 'exp')), may hold values from -6 to 6
- kv_pool: bfloat16 [32, 16, 32, 16, 1024], P('req', 'exp'), may hold values from -6 to 6
- block_table: int32 [2048, 8], P(('req', 'exp')), may hold values from 0 to 31, as said below
- lengths: int32 [2048], P(('req', 'exp')), may hold values from 1 to 128, as said below
- mig_source: int32 [32, 16, 2, 4], P('req', 'exp'), may hold values from 0 to 31, as said below
- mig_target: int32 [32, 16, 2, 4], P('req', 'exp'), may hold values from 0 to 31, as said below
- expert_ids: int32 [4096, 8], P('req'), may hold values from 0 to 63, all different within a row; in each aligned block of 128 rows (0 to 127, 128 to 255, ...) at most 24 rows name the same one
- gate_values: float32 [4096, 8], P('req'), may hold values from 0.2 to 1
- norm_gain: bfloat16 [3584], replicated, may hold values from 0.5 to 1.5
- w_in: bfloat16 [16, 32, 3584, 256], P('exp', 'req'), may hold values from -0.09375 to 0.09375
- w_out: bfloat16 [16, 32, 256, 3584], P('exp', 'req'), may hold values from -0.125 to 0.125
Outputs:
- mixed: bfloat16 [4096, 3584], P(('req', 'exp'))
Inputs may be any that keep to these rules, and one draw needn't show every extreme that they name: `block_table`: the entries of the 4 rows of one device are distinct pages of that device's pool. `lengths`: A request that arrives by migration has more than (3) * 16 cached positions. `mig_target`: on every device exactly one request arrives from req index - 1 and one from index + 1 (around the loop); [r, e, 0, i] is the page that takes page i of the request from index - 1, [r, e, 1, i] of the one from index + 1; they are the first 4 entries of that request's block-table row. `mig_source`: [r, e, 0, i] is the pool page sent as page i to index + 1, [r, e, 1, i] to index - 1; the 8 pages of a device are distinct and belong to no request that stays on it. `expert_ids`: each row names 8 different experts; among the 128 tokens of one index of req no expert is named by more than 24 rows.
All inputs are finite; a program needn't handle non-finite values.
Results may differ from a plain program's by a relative error of at most 0.012.
Values may be sent and summed in bfloat16 or wider, within the bound.
A program may use at most 64 MiB of HBM per device.

v0:
```python
import jax
import jax.numpy as jnp
from jax import lax
from jax.sharding import PartitionSpec as P

HEADS = 28
KV_HEADS = 4
HEAD_DIM = 128
EXP_DEV = 4
CAP = 24
neg_big = -1e30
norm_eps = 1e-06


def with_halo(block, sides, width):
    for axis, dim in sides:
        count = lax.axis_size(axis)
        forward = [(i, i + 1) for i in range(count - 1)]
        forward.append((count - 1, 0))
        backward = [(target, source) for source, target in forward]
        low = lax.ppermute(
            lax.slice_in_dim(block, block.shape[dim] - width, None, axis=dim), axis, forward
        )
        high = lax.ppermute(lax.slice_in_dim(block, 0, width, axis=dim), axis, backward)
        block = jnp.concatenate([low, block, high], axis=dim)
    return block


def partial_attention(query_grid, key_rows, visible):
    request_count = key_rows.shape[0]
    span = key_rows.shape[1]
    key_width = KV_HEADS * HEAD_DIM
    key_part = key_rows[:, :, :key_width].reshape(request_count, span, KV_HEADS, HEAD_DIM)
    value_part = (
        key_rows[:, :, key_width:]
        .reshape(request_count, span, KV_HEADS, HEAD_DIM)
        .astype(jnp.float32)
    )
    scores = jnp.einsum(
        "rdkgh,rpkh->rdkgp", query_grid, key_part, preferred_element_type=jnp.float32
    ) * HEAD_DIM ** (-0.5)
    live = visible[:, :, None, None, :]
    scores = jnp.where(live, scores, neg_big)
    highest = jnp.max(scores, axis=-1)
    weights = jnp.where(live, jnp.exp(scores - highest[..., None]), 0.0)
    weight_sum = jnp.sum(weights, axis=-1)
    summed = jnp.einsum("rdkgp,rpkh->rdkgh", weights, value_part, precision=lax.Precision.HIGHEST)
    return (highest, weight_sum, summed)


def body(
    resid_in,
    queries,
    fresh_kv,
    kv_pool,
    block_table,
    lengths,
    mig_source,
    mig_target,
    expert_ids,
    gate_values,
    norm_gain,
    w_in,
    w_out,
):
    request_count = block_table.shape[0]
    table_width = block_table.shape[1]
    page_tokens = kv_pool.shape[3]
    kv_width = kv_pool.shape[4]
    cache_span = table_width * page_tokens
    token_count = resid_in.shape[0]
    draft_count = token_count // request_count
    model_width = resid_in.shape[1]
    moved = mig_source.shape[3]
    pool_pages = kv_pool[0, 0]
    sources = mig_source[0, 0]
    target_pairs = mig_target[0, 0]
    outgoing = jnp.concatenate([pool_pages[sources[1]], pool_pages[sources[0]]], axis=0)
    targets = jnp.concatenate([target_pairs[0], target_pairs[1]], axis=0)
    extended = with_halo(outgoing, (("req", 0),), moved)
    arrivals = jnp.concatenate([extended[:moved], extended[-moved:]], axis=0)
    query_grid = queries.reshape(request_count, draft_count, KV_HEADS, HEADS // KV_HEADS, HEAD_DIM)
    fresh_rows = fresh_kv.reshape(request_count, draft_count, kv_width)
    position = jnp.arange(cache_span)
    cache_visible = jnp.broadcast_to(
        position[None, None, :] < lengths[:, None, None], (request_count, draft_count, cache_span)
    )
    draft_index = jnp.arange(draft_count)
    draft_visible = jnp.broadcast_to(
        draft_index[None, :] <= draft_index[:, None], (request_count, draft_count, draft_count)
    )
    pool_after = pool_pages.at[targets].set(arrivals)
    cache_rows = pool_after[block_table].reshape(request_count, cache_span, kv_width)
    parts = partial_attention(
        query_grid,
        jnp.concatenate([cache_rows, fresh_rows], axis=1),
        jnp.concatenate([cache_visible, draft_visible], axis=2),
    )
    attention = (parts[2] / parts[1][..., None]).reshape(token_count, model_width)
    residual = resid_in.astype(jnp.float32) + attention
    inv_rms = lax.rsqrt(jnp.mean(residual * residual, axis=1, keepdims=True) + norm_eps)
    normed = (residual * inv_rms * norm_gain.astype(jnp.float32)).astype(jnp.bfloat16)
    local_ids = lax.axis_index("exp") * EXP_DEV + jnp.arange(EXP_DEV)
    matches = expert_ids[None, :, :] == local_ids[:, None, None]
    is_named = jnp.any(matches, axis=2)
    gate_local = jnp.sum(jnp.where(matches, gate_values[None, :, :], 0.0), axis=2)
    slot_index = jnp.cumsum(is_named.astype(jnp.int32), axis=1) - 1
    placement = is_named[:, None, :] & (slot_index[:, None, :] == jnp.arange(CAP)[None, :, None])
    slot_gate = jnp.sum(jnp.where(placement, gate_local[:, None, :], 0.0), axis=2)
    slot_select = placement.astype(jnp.bfloat16)
    columns = slot_select
    packed = jnp.einsum(
        "kct,td->kcd",
        columns,
        lax.all_gather(normed, "exp", axis=0, tiled=True),
        preferred_element_type=jnp.float32,
    )
    packed = packed.astype(jnp.bfloat16)
    group_size = lax.axis_size("req") // EXP_DEV
    outbound = jnp.repeat(packed, group_size, axis=0)
    inner_weights = w_in[0, 0]
    outer_weights = w_out[0, 0]
    inbound = lax.all_to_all(outbound, "req", split_axis=0, concat_axis=0, tiled=True)
    hidden = jnp.einsum("scd,df->scf", inbound, inner_weights, preferred_element_type=jnp.float32)
    activated = jax.nn.silu(hidden).astype(jnp.bfloat16)
    returned = lax.all_to_all(
        jnp.einsum(
            "scf,fd->scd", activated, outer_weights, preferred_element_type=jnp.float32
        ).astype(jnp.bfloat16),
        "req",
        split_axis=0,
        concat_axis=0,
        tiled=True,
    )
    expert_out = jnp.sum(
        returned.reshape(EXP_DEV, group_size, CAP, model_width).astype(jnp.float32), axis=1
    )
    weighted = expert_out * slot_gate[:, :, None]
    slot_select_wide = placement.astype(jnp.float32)
    columns = slot_select_wide
    expert_mix = lax.psum_scatter(
        jnp.einsum("kct,kcd->td", columns, weighted, precision=lax.Precision.HIGHEST).astype(
            jnp.bfloat16
        ),
        "exp",
        scatter_dimension=0,
        tiled=True,
    ).astype(jnp.float32)
    return (residual + expert_mix).astype(jnp.bfloat16)


def solution(mesh):
    placed = (
        P(("req", "exp"), None),
        P(("req", "exp"), None),
        P(("req", "exp"), None),
        P("req", "exp", None, None, None),
        P(("req", "exp"), None),
        P(("req", "exp")),
        P("req", "exp", None, None),
        P("req", "exp", None, None),
        P("req", None),
        P("req", None),
        P(),
        P("exp", "req", None, None),
        P("exp", "req", None, None),
    )
    return jax.shard_map(
        body, mesh=mesh, in_specs=placed, out_specs=P(("req", "exp"), None), check_vma=False
    )
```

profile of v0, /device:TPU:2, one launch (start us, length us, event | category | flops | bytes accessed | tf_op | source)
XLA Modules:
  0.0 401.4 jit_solution(36043764672212285)
XLA Ops:
  6.6 1.4 copy.45
  8.0 0.6 gather_fusion
  8.5 3.4 collective-permute-start
  11.9 0.6 gather_fusion.1
  12.5 6.3 %collective-permute-start.1 = (bf16[4,16,1024]{2,1,0:T(8,128)(2,1)S(1)}, bf16[4,16,1024]{2,1,0:T(8,128)(2,1)S(1)}, u32[]{:S(2)}, u32[]{:S(2)}) collective-permute-start(bf16[4,16,1024]{2,1,0:T(8,128)(2,1)S(1)} %gather_fusion.1), channel_id=1, source_target_pairs={{16,0},{32,16},{48,32},{64,48},{80,64},{96,80},{112,96},{128,112},... | collective-permute-start | bytes 393224 | tf_op jit(solution)/shard_map/ppermute | solution.py:24
  19.0 0.6 pad_clamp_fusion
  19.6 0.7 iota_compare_fusion.1
  21.2 0.6 fusion.31
  21.9 1.3 convert_element_type.45
  23.2 0.7 broadcast_in_dim.77
  24.0 0.9 scatter_fusion
  24.9 1.7 gather_fusion.2
  26.6 1.3 pad_maximum_fusion
  28.3 0.5 fusion.36
  29.0 0.6 fusion.7
  30.0 21.8 %all_gather.3 = bf16[128,3584]{1,0:T(8,128)(2,1)S(1)} all-gather(bf16[8,3584]{1,0:T(8,128)(2,1)S(1)} %multiply_convert_fusion.1), channel_id=1, replica_groups=mesh['req'=32,'exp'=16] {'exp'}, dimensions={0}, use_global_device_ids=true | all-gather | bytes 974848 | tf_op jit(solution)/shard_map/all_gather | solution.py:115
  52.5 135.6 %all_to_all.10 = bf16[32,24,3584]{2,1,0:T(8,128)(2,1)} all-to-all(bf16[32,24,3584]{2,1,0:T(8,128)(2,1)S(1)} %bitcast.52), channel_id=1, replica_groups=mesh['req'=32,'exp'=16] {'req'}, dimensions={0} | all-to-all | bytes 11010048 | tf_op jit(solution)/shard_map/all_to_all | solution.py:123
  188.1 11.5 %convolution_convert_fusion = bf16[32,24,3584]{2,1,0:T(8,128)(2,1)} fusion(bf16[1,1,256,3584]{3,2,1,0:T(8,128)(2,1)S(1)} %copy-done, bf16[32,24,3584]{2,1,0:T(8,128)(2,1)} %all_to_all.10, bf16[1,1,3584,256]{3,2,1,0:T(8,128)(2,1)} %param.24), kind=kOutput, calls=%fused_computation.5 | convolution fusion | flops 2822307840 | bytes 14680064 | tf_op jit(solution)/shard_map/scf,fd->scd/dot_general | solution.py:127
  199.6 6.3 %all-to-all-start.1 = ((bf16[32,24,3584]{2,1,0:T(8,128)(2,1)}), bf16[32,24,3584]{2,1,0:T(8,128)(2,1)}, u32[]{:S(2)}, u32[]{:S(2)}) async-start(bf16[32,24,3584]{2,1,0:T(8,128)(2,1)} %convolution_convert_fusion), calls=%async_computation.1 | async-start | bytes 11010048 | tf_op jit(solution)/shard_map/all_to_all | solution.py:126
  206.2 125.1 %all-to-all-done.1 = bf16[32,24,3584]{2,1,0:T(8,128)(2,1)} async-done(((bf16[32,24,3584]{2,1,0:T(8,128)(2,1)}), bf16[32,24,3584]{2,1,0:T(8,128)(2,1)}, u32[]{:S(2)}, u32[]{:S(2)}) %all-to-all-start.1) | async-done | bytes 5505056 | tf_op jit(solution)/shard_map/all_to_all | solution.py:126
  331.3 3.5 convert_reduce_fusion
  334.8 2.0 fusion
  336.8 56.4 %reduce-scatter.2.cloned.1.call-done = bf16[8,3584]{1,0:T(8,128)(2,1)} async-done(((bf16[128,3584]{1,0:T(8,128)(2,1)}), bf16[8,3584]{1,0:T(8,128)(2,1)}) %reduce-scatter.2.cloned.1.call-update) | async-done | bytes 57360 | tf_op jit(solution)/shard_map/reduce_scatter | solution.py:141
  393.1 1.5 add_convert_fusion
  (65 shorter events, 3.1 us)
Async XLA Ops:
  6.5 181.5 %copy-start = (bf16[1,1,256,3584]{3,2,1,0:T(8,128)(2,1)S(1)}, bf16[1,1,256,3584]{3,2,1,0:T(8,128)(2,1)}, u32[]{:S(2)}) copy-start(bf16[1,1,256,3584]{3,2,1,0:T(8,128)(2,1)} %param.25) | copy-start | bytes 5505028
  6.5 15.3 %copy-start.3 = (bf16[8,3584]{1,0:T(8,128)(2,1)S(1)}, bf16[8,3584]{1,0:T(8,128)(2,1)}, u32[]{:S(2)}) copy-start(bf16[8,3584]{1,0:T(8,128)(2,1)} %param.14) | copy-start | bytes 172036
  6.5 15.3 %copy-start.6 = (bf16[8,1024]{1,0:T(8,128)(2,1)S(1)}, bf16[8,1024]{1,0:T(8,128)(2,1)}, u32[]{:S(2)}) copy-start(bf16[8,1024]{1,0:T(8,128)(2,1)} %param.15) | copy-start | bytes 49156
  6.5 12.3 %copy-start.10 = (s32[4,8]{1,0:T(4,128)S(1)}, s32[4,8]{1,0:T(4,128)}, u32[]{:S(2)}) copy-start(s32[4,8]{1,0:T(4,128)} %param.17) | copy-start | bytes 388
  6.5 13.0 %copy-start.15 = (s32[4]{0:T(128)S(1)}, s32[4]{0:T(128)}, u32[]{:S(2)}) copy-start(s32[4]{0:T(128)} %param.18) | copy-start | bytes 52
  6.5 1.4 copy-start.13
  6.6 12.3 %copy-start.14 = (s32[1,1,2,4]{3,2,1,0:T(2,128)S(1)}, s32[1,1,2,4]{3,2,1,0:T(2,128)}, u32[]{:S(2)}) copy-start(s32[1,1,2,4]{3,2,1,0:T(2,128)} %param.20) | copy-start | bytes 100
  6.6 13.7 %copy-start.4 = (s32[128,8]{0,1:T(8,128)S(1)}, s32[128,8]{0,1:T(8,128)}, u32[]{:S(2)}) copy-start(s32[128,8]{0,1:T(8,128)} %param.21) | copy-start | bytes 12292
  8.5 15.4 %collective-permute-start = (bf16[4,16,1024]{2,1,0:T(8,128)(2,1)S(1)}, bf16[4,16,1024]{2,1,0:T(8,128)(2,1)S(1)}, u32[]{:S(2)}, u32[]{:S(2)}) collective-permute-start(bf16[4,16,1024]{2,1,0:T(8,128)(2,1)S(1)} %gather_fusion), channel_id=1, source_target_pairs={{0,16},{16,32},{32,48},{48,64},{64,80},{80,96},{96,112},{112,128},... | collective-permute-start | bytes 393224 | tf_op jit(solution)/shard_map/ppermute | solution.py:21
  12.5 11.4 %collective-permute-start.1 = (bf16[4,16,1024]{2,1,0:T(8,128)(2,1)S(1)}, bf16[4,16,1024]{2,1,0:T(8,128)(2,1)S(1)}, u32[]{:S(2)}, u32[]{:S(2)}) collective-permute-start(bf16[4,16,1024]{2,1,0:T(8,128)(2,1)S(1)} %gather_fusion.1), channel_id=1, source_target_pairs={{16,0},{32,16},{48,32},{64,48},{80,64},{96,80},{112,96},{128,112},... | collective-permute-start | bytes 393224 | tf_op jit(solution)/shard_map/ppermute | solution.py:24
  20.2 0.5 copy-start.11
  20.7 0.5 copy-start.7
  28.3 1.4 copy-start.1
  28.3 1.6 copy-start.2
  29.0 22.8 %copy-start.8 = (pred[4,128]{1,0:T(4,128)(4,1)S(1)}, pred[4,128]{1,0:T(4,128)(4,1)}, u32[]{:S(2)}) copy-start(pred[4,128]{1,0:T(4,128)(4,1)} %copy-done.7) | copy-start | bytes 1540
  199.6 6.4 %copy-start.5 = (s32[128,8]{0,1:T(8,128)S(1)}, s32[128,8]{0,1:T(8,128)}, u32[]{:S(2)}) copy-start(s32[128,8]{0,1:T(8,128)} %param.21) | copy-start | bytes 12292
  199.6 6.4 %copy-start.9 = (f32[128,8]{0,1:T(8,128)S(1)}, f32[128,8]{0,1:T(8,128)}, u32[]{:S(2)}) copy-start(f32[128,8]{0,1:T(8,128)} %param.22) | copy-start | bytes 12292
  199.6 6.4 %copy-start.12 = (s32[4]{0:T(128)S(1)}, s32[4]{0:T(128)}, u32[]{:S(2)}) copy-start(s32[4]{0:T(128)} %copy-done.11) | copy-start | bytes 52
  199.6 131.7 %all-to-all-start.1 = ((bf16[32,24,3584]{2,1,0:T(8,128)(2,1)}), bf16[32,24,3584]{2,1,0:T(8,128)(2,1)}, u32[]{:S(2)}, u32[]{:S(2)}) async-start(bf16[32,24,3584]{2,1,0:T(8,128)(2,1)} %convolution_convert_fusion), calls=%async_computation.1 | async-start | bytes 11010048 | tf_op jit(solution)/shard_map/all_to_all | solution.py:126
  205.9 187.2 %reduce-scatter.2.cloned.1.call-start = ((), (), s32[]{:S(2)}) async-start(), calls=%async_computation.3 | async-start | bytes 974848 | tf_op jit(solution)/shard_map/reduce_scatter | solution.py:141
Sparse Core Ops, SparseCore 0:
  336.9 56.1 reduce-scatter.1
where the time goes:
time: 402 us; the launch traced here: 401 us
  waiting for transfers between devices  182 us (45%)
  blocking collectives  157 us (39%)
  starting transfers between devices  16 us (4%)
  matrix products  14.9 us (4%)
  between operations  13.7 us (3%)
  other arithmetic  10.5 us (3%)
  local copies, waits for them, and re-layouts  7.34 us (2%)
    all_to_all x1, blocking collectives, body(): lax.all_to_all(outbound, 'req', split_axis=0, concat_axis=0, tiled=True)  136 us
    all_to_all x1, waiting for transfers between devices, body(): lax.all_to_all(jnp.einsum('scf,fd->scd', activated, outer_weights, prefer...  125 us
    reduce_scatter x1, waiting for transfers between devices, body(): lax.psum_scatter(jnp.einsum('kct,kcd->td', columns, weighted, precision=l...  56.4 us
    all_gather x1, blocking collectives, body(): lax.all_gather(normed, 'exp', axis=0, tiled=True)  21.8 us
    dot_general x1, matrix products, body(): jnp.einsum('scf,fd->scd', activated, outer_weights, preferred_element_typ...  11.5 us
  transfers between devices with their start and end apart: 4, of which 2 were waited for; matrix products, arithmetic and copies ran while one was open for 1% of the time, Pallas kernels for 0%

commit v1 on v0

--- a/solution.py
+++ b/solution.py
@@ -112,7 +112,9 @@
     packed = jnp.einsum(
         "kct,td->kcd",
         columns,
-        lax.all_gather(normed, "exp", axis=0, tiled=True),
+        jnp.concatenate(
+            lax.all_to_all(jnp.stack([normed] * lax.axis_size("exp")), "exp", 0, 0), axis=0
+        ),
         preferred_element_type=jnp.float32,
     )
     packed = packed.astype(jnp.bfloat16)

time: 402 us -> 416 us (1.035)
  waiting for transfers between devices: 182 us -> 209 us
  blocking collectives: 157 us -> 136 us
  starting transfers between devices: 16 us -> 24.6 us
    all_to_all x0 -> x1, waiting for transfers between devices: none -> 22.7 us  [body(): lax.all_to_all(jnp.stack([normed] * lax.axis_size('exp')), 'exp', 0, 0)]
    all_gather x1 -> x0, blocking collectives: 21.8 us -> none  [body(): lax.all_gather(normed, 'exp', axis=0, tiled=True)]
    all_to_all x0 -> x1, starting transfers between devices: none -> 8.47 us  [body(): lax.all_to_all(jnp.stack([normed] * lax.axis_size('exp')), 'exp', 0, 0)]
  transfers between devices with their start and end apart: 4 -> 5, of which waited for: 2 -> 4; matrix products, arithmetic and copies ran while one was open for 1% -> 1% of each run, Pallas kernels for 0% -> 0%
where the time goes in v1:
time: 416 us
  waiting for transfers between devices  209 us (50%)
  blocking collectives  136 us (33%)
  starting transfers between devices  24.6 us (6%)
  matrix products  16.5 us (4%)
  between operations  13.7 us (3%)
  other arithmetic  8.81 us (2%)
  local copies, waits for them, and re-layouts  7.43 us (2%)
    all_to_all x1, blocking collectives, body(): lax.all_to_all(outbound, 'req', split_axis=0, concat_axis=0, tiled=True)  136 us
    all_to_all x1, waiting for transfers between devices, body(): lax.all_to_all(jnp.einsum('scf,fd->scd', activated, outer_weights, prefer...  128 us
    reduce_scatter x1, waiting for transfers between devices, body(): lax.psum_scatter(jnp.einsum('kct,kcd->td', columns, weighted, precision=l...  57.2 us
    all_to_all x1, waiting for transfers between devices, body(): lax.all_to_all(jnp.stack([normed] * lax.axis_size('exp')), 'exp', 0, 0)  22.7 us
    dot_general x1, matrix products, body(): jnp.einsum('scf,fd->scd', activated, outer_weights, preferred_element_typ...  11.5 us
    all_to_all x1, starting transfers between devices, body(): lax.all_to_all(jnp.stack([normed] * lax.axis_size('exp')), 'exp', 0, 0)  8.47 us
  transfers between devices with their start and end apart: 5, of which 4 were waited for; matrix products, arithmetic and copies ran while one was open for 1% of the time, Pallas kernels for 0%

profile of v1, /device:TPU:2, one launch (start us, length us, event | category | flops | bytes accessed | tf_op | source)
XLA Modules:
  0.0 415.8 jit_solution(5644534001552788848)
XLA Ops:
  6.6 1.4 copy.45
  7.9 0.6 gather_fusion
  8.5 3.4 collective-permute-start
  12.5 6.3 %collective-permute-start.1 = (bf16[4,16,1024]{2,1,0:T(8,128)(2,1)S(1)}, bf16[4,16,1024]{2,1,0:T(8,128)(2,1)S(1)}, u32[]{:S(2)}, u32[]{:S(2)}) collective-permute-start(bf16[4,16,1024]{2,1,0:T(8,128)(2,1)S(1)} %gather_fusion.1), channel_id=1, source_target_pairs={{16,0},{32,16},{48,32},{64,48},{80,64},{96,80},{112,96},{128,112},... | collective-permute-start | bytes 393224 | tf_op jit(solution)/shard_map/ppermute | solution.py:24
  19.1 0.7 reshape.233
  19.9 0.6 pad_add_fusion
  20.5 0.8 collective-permute-done.1
  21.3 0.8 scatter_fusion
  22.1 1.6 gather_fusion.2
  23.7 1.3 pad_maximum_fusion
  25.4 1.3 fusion.36
  26.8 0.9 fusion.18
  27.7 1.3 fusion.7
  29.3 1.0 stack.2
  30.3 8.5 %all-to-all-start = ((bf16[16,8,3584]{2,1,0:T(8,128)(2,1)}), bf16[16,8,3584]{2,1,0:T(8,128)(2,1)S(1)}, u32[]{:S(2)}, u32[]{:S(2)}) async-start(bf16[16,8,3584]{2,1,0:T(8,128)(2,1)} %stack.2), calls=%async_computation | async-start | bytes 1835008 | tf_op jit(solution)/shard_map/all_to_all | solution.py:116
  39.2 22.7 %all-to-all-done = bf16[16,8,3584]{2,1,0:T(8,128)(2,1)S(1)} async-done(((bf16[16,8,3584]{2,1,0:T(8,128)(2,1)}), bf16[16,8,3584]{2,1,0:T(8,128)(2,1)S(1)}, u32[]{:S(2)}, u32[]{:S(2)}) %all-to-all-start) | async-done | bytes 917536 | tf_op jit(solution)/shard_map/all_to_all | solution.py:116
  62.6 135.6 %all_to_all.15 = bf16[32,24,3584]{2,1,0:T(8,128)(2,1)} all-to-all(bf16[32,24,3584]{2,1,0:T(8,128)(2,1)S(1)} %bitcast.54), channel_id=1, replica_groups=mesh['req'=32,'exp'=16] {'req'}, dimensions={0} | all-to-all | bytes 11010048 | tf_op jit(solution)/shard_map/all_to_all | solution.py:125
  198.2 11.5 %convolution_convert_fusion = bf16[32,24,3584]{2,1,0:T(8,128)(2,1)} fusion(bf16[1,1,256,3584]{3,2,1,0:T(8,128)(2,1)S(1)} %copy-done, bf16[32,24,3584]{2,1,0:T(8,128)(2,1)} %all_to_all.15, bf16[1,1,3584,256]{3,2,1,0:T(8,128)(2,1)} %param.24), kind=kOutput, calls=%fused_computation.5 | convolution fusion | flops 2822307840 | bytes 14680064 | tf_op jit(solution)/shard_map/scf,fd->scd/dot_general | solution.py:129
  209.8 6.4 %all-to-all-start.2 = ((bf16[32,24,3584]{2,1,0:T(8,128)(2,1)}), bf16[32,24,3584]{2,1,0:T(8,128)(2,1)}, u32[]{:S(2)}, u32[]{:S(2)}) async-start(bf16[32,24,3584]{2,1,0:T(8,128)(2,1)} %convolution_convert_fusion), calls=%async_computation.2 | async-start | bytes 11010048 | tf_op jit(solution)/shard_map/all_to_all | solution.py:128
  216.4 128.5 %all-to-all-done.2 = bf16[32,24,3584]{2,1,0:T(8,128)(2,1)} async-done(((bf16[32,24,3584]{2,1,0:T(8,128)(2,1)}), bf16[32,24,3584]{2,1,0:T(8,128)(2,1)}, u32[]{:S(2)}, u32[]{:S(2)}) %all-to-all-start.2) | async-done | bytes 5505056 | tf_op jit(solution)/shard_map/all_to_all | solution.py:128
  344.9 3.5 convert_reduce_fusion
  348.3 2.0 fusion
  350.3 57.2 %reduce-scatter.2.cloned.1.call-done = bf16[8,3584]{1,0:T(8,128)(2,1)} async-done(((bf16[128,3584]{1,0:T(8,128)(2,1)}), bf16[8,3584]{1,0:T(8,128)(2,1)}) %reduce-scatter.2.cloned.1.call-update) | async-done | bytes 57360 | tf_op jit(solution)/shard_map/reduce_scatter | solution.py:143
  407.5 1.5 add_convert_fusion
  (57 shorter events, 2.9 us)
Async XLA Ops:
  6.5 191.7 %copy-start = (bf16[1,1,256,3584]{3,2,1,0:T(8,128)(2,1)S(1)}, bf16[1,1,256,3584]{3,2,1,0:T(8,128)(2,1)}, u32[]{:S(2)}) copy-start(bf16[1,1,256,3584]{3,2,1,0:T(8,128)(2,1)} %param.25) | copy-start | bytes 5505028
  6.5 12.6 %copy-start.2 = (bf16[8,3584]{1,0:T(8,128)(2,1)S(1)}, bf16[8,3584]{1,0:T(8,128)(2,1)}, u32[]{:S(2)}) copy-start(bf16[8,3584]{1,0:T(8,128)(2,1)} %param.14) | copy-start | bytes 172036
  6.5 12.6 %copy-start.4 = (bf16[8,1024]{1,0:T(8,128)(2,1)S(1)}, bf16[8,1024]{1,0:T(8,128)(2,1)}, u32[]{:S(2)}) copy-start(bf16[8,1024]{1,0:T(8,128)(2,1)} %param.15) | copy-start | bytes 49156
  6.5 12.3 %copy-start.7 = (s32[4,8]{1,0:T(4,128)S(1)}, s32[4,8]{1,0:T(4,128)}, u32[]{:S(2)}) copy-start(s32[4,8]{1,0:T(4,128)} %param.17) | copy-start | bytes 388
  6.5 12.4 %copy-start.10 = (s32[4]{0:T(128)S(1)}, s32[4]{0:T(128)}, u32[]{:S(2)}) copy-start(s32[4]{0:T(128)} %param.18) | copy-start | bytes 52
  6.5 1.4 copy-start.8
  6.6 12.3 %copy-start.9 = (s32[1,1,2,4]{3,2,1,0:T(2,128)S(1)}, s32[1,1,2,4]{3,2,1,0:T(2,128)}, u32[]{:S(2)}) copy-start(s32[1,1,2,4]{3,2,1,0:T(2,128)} %param.20) | copy-start | bytes 100
  6.6 13.3 %copy-start.5 = (bf16[3584]{0:T(1024)(128)(2,1)S(1)}, bf16[3584]{0:T(1024)(128)(2,1)}, u32[]{:S(2)}) copy-start(bf16[3584]{0:T(1024)(128)(2,1)} %param.23) | copy-start | bytes 21508
  8.5 12.0 %collective-permute-start = (bf16[4,16,1024]{2,1,0:T(8,128)(2,1)S(1)}, bf16[4,16,1024]{2,1,0:T(8,128)(2,1)S(1)}, u32[]{:S(2)}, u32[]{:S(2)}) collective-permute-start(bf16[4,16,1024]{2,1,0:T(8,128)(2,1)S(1)} %gather_fusion), channel_id=1, source_target_pairs={{0,16},{16,32},{32,48},{48,64},{64,80},{80,96},{96,112},{112,128},... | collective-permute-start | bytes 393224 | tf_op jit(solution)/shard_map/ppermute | solution.py:21
  12.5 8.8 %collective-permute-start.1 = (bf16[4,16,1024]{2,1,0:T(8,128)(2,1)S(1)}, bf16[4,16,1024]{2,1,0:T(8,128)(2,1)S(1)}, u32[]{:S(2)}, u32[]{:S(2)}) collective-permute-start(bf16[4,16,1024]{2,1,0:T(8,128)(2,1)S(1)} %gather_fusion.1), channel_id=1, source_target_pairs={{16,0},{32,16},{48,32},{64,48},{80,64},{96,80},{112,96},{128,112},... | collective-permute-start | bytes 393224 | tf_op jit(solution)/shard_map/ppermute | solution.py:24
  25.4 3.7 copy-start.1
  29.0 9.8 %copy-start.3 = (s32[128,8]{0,1:T(8,128)S(1)}, s32[128,8]{0,1:T(8,128)}, u32[]{:S(2)}) copy-start(s32[128,8]{0,1:T(8,128)} %param.21) | copy-start | bytes 12292
  30.3 31.6 %all-to-all-start = ((bf16[16,8,3584]{2,1,0:T(8,128)(2,1)}), bf16[16,8,3584]{2,1,0:T(8,128)(2,1)S(1)}, u32[]{:S(2)}, u32[]{:S(2)}) async-start(bf16[16,8,3584]{2,1,0:T(8,128)(2,1)} %stack.2), calls=%async_computation | async-start | bytes 1835008 | tf_op jit(solution)/shard_map/all_to_all | solution.py:116
  209.8 6.4 %copy-start.6 = (f32[128,8]{0,1:T(8,128)S(1)}, f32[128,8]{0,1:T(8,128)}, u32[]{:S(2)}) copy-start(f32[128,8]{0,1:T(8,128)} %param.22) | copy-start | bytes 12292
  209.8 135.1 %all-to-all-start.2 = ((bf16[32,24,3584]{2,1,0:T(8,128)(2,1)}), bf16[32,24,3584]{2,1,0:T(8,128)(2,1)}, u32[]{:S(2)}, u32[]{:S(2)}) async-start(bf16[32,24,3584]{2,1,0:T(8,128)(2,1)} %convolution_convert_fusion), calls=%async_computation.2 | async-start | bytes 11010048 | tf_op jit(solution)/shard_map/all_to_all | solution.py:128
  216.1 191.4 %reduce-scatter.2.cloned.1.call-start = ((), (), s32[]{:S(2)}) async-start(), calls=%async_computation.4 | async-start | bytes 974848 | tf_op jit(solution)/shard_map/reduce_scatter | solution.py:143
Sparse Core Ops, SparseCore 0:
  350.4 57.0 reduce-scatter.1
